TPU v7x, 256 devices: a whole 4x4x8 slice. The times are simulated.
256 devices in a mesh: span: 8 (over z), ha: 8 (over x, core), wa: 4 (over y).
Axes of the slice: x: 4, y: 4, z: 8, core: 2. Of those that a mesh axis runs over, the one named last changes fastest.
Arguments:
- queries: bfloat16 [8, 3, 32, 48, 768], P('span', None, 'ha', 'wa'), may hold values from -5 to 5
- cache_keys: bfloat16 [8, 3, 32, 48, 768], P('span', None, 'ha', 'wa'), may hold values from -5 to 5
- cache_values: bfloat16 [8, 3, 32, 48, 768], P('span', None, 'ha', 'wa'), may hold values from -16 to 16
- grad_attended: bfloat16 [8, 3, 32, 48, 768], P('span', None, 'ha', 'wa'), may hold values from -16 to 16
- radius: int32 [6], replicated, may hold values from 1 to 2, as said below
- frame_count: int32 [8], replicated, may hold values from 1 to 3, as said below
Outputs:
- attended: bfloat16 [8, 3, 32, 48, 768], P('span', None, 'ha', 'wa')
- grad_queries: bfloat16 [8, 3, 32, 48, 768], P('span', None, 'ha', 'wa')
- grad_keys: bfloat16 [8, 3, 32, 48, 768], P('span', None, 'ha', 'wa')
- grad_values: bfloat16 [8, 3, 32, 48, 768], P('span', None, 'ha', 'wa')
Inputs may be any that keep to these rules, and one draw needn't show every extreme that they name: Some head has radius 2 and some other head has radius 1. Frame slots of block c at or past frame_count[c] hold padding; some block has all 3 slots live.
All inputs are finite; a program needn't handle non-finite values.
Results may differ from a plain program's by a relative error of at most 0.02.
Values may be sent and summed in bfloat16 or wider, within the bound.
A program may use at most 128 MiB of HBM per device.

v0:
```python
import math
import jax
import jax.numpy as jnp
from jax import lax
from jax.sharding import PartitionSpec as P

RMAX = 2


def padded(block, sides, width):
    for axis, dim in sides:
        count = lax.axis_size(axis)
        forward = [(i, i + 1) for i in range(count - 1)]
        backward = [(target, source) for source, target in forward]
        low = lax.ppermute(
            lax.slice_in_dim(block, block.shape[dim] - width, None, axis=dim), axis, forward
        )
        high = lax.ppermute(lax.slice_in_dim(block, 0, width, axis=dim), axis, backward)
        block = jnp.concatenate([low, block, high], axis=dim)
    return block


def near_table(radius, tile_h, tile_w, margin, first_row, first_col, full_h, full_w):
    rows_local = jnp.arange(tile_h)
    rows_wide = jnp.arange(tile_h + 2 * margin) - margin
    cols_local = jnp.arange(tile_w)
    cols_wide = jnp.arange(tile_w + 2 * margin) - margin
    gap_rows = jnp.abs(rows_local[:, None] - rows_wide[None, :])
    gap_cols = jnp.abs(cols_local[:, None] - cols_wide[None, :])
    inside_rows = (first_row + rows_wide >= 0) & (first_row + rows_wide < full_h)
    inside_cols = (first_col + cols_wide >= 0) & (first_col + cols_wide < full_w)
    reach = jnp.maximum(gap_rows[:, None, :, None], gap_cols[None, :, None, :])
    inside = inside_rows[:, None] & inside_cols[None, :]
    within = (reach[None] <= radius[:, None, None, None, None]) & inside[None, None, None]
    return within.reshape(
        radius.shape[0], tile_h * tile_w, (tile_h + 2 * margin) * (tile_w + 2 * margin)
    )


def with_frames(spatial, frame_live):
    heads, rows, columns = spatial.shape
    frames = frame_live.shape[0]
    joined = spatial[:, None, :, None, :] & frame_live[None, None, None, :, None]
    joined = jnp.broadcast_to(joined, (heads, frames, rows, frames, columns))
    return joined.reshape(heads, frames * rows, frames * columns)


def live_frames(frame_count, block_id, frames):
    picked = jnp.arange(frame_count.shape[0]) == block_id
    count = jnp.sum(jnp.where(picked, frame_count, 0))
    return jnp.arange(frames) < count


def over_tiles(advance, carried, piece):
    block_ids = jnp.arange(piece.shape[0], dtype=jnp.int32)

    def inner(current, item):
        return (advance(current, item[0], item[1]), None)

    result, _ = lax.scan(inner, carried, (piece, block_ids))
    return result


def shards(queries, cache_keys, cache_values, grad_attended, radius, frame_count):
    frames, tile_h, tile_w, width = queries.shape[1:]
    heads = radius.shape[0]
    depth = width // heads
    margin = RMAX
    scale = 1.0 / math.sqrt(depth)
    own_block = lax.axis_index("span")
    block_total = lax.axis_size("span")
    first_row = lax.axis_index("ha") * tile_h
    first_col = lax.axis_index("wa") * tile_w
    spatial = near_table(
        radius,
        tile_h,
        tile_w,
        margin,
        first_row,
        first_col,
        tile_h * lax.axis_size("ha"),
        tile_w * lax.axis_size("wa"),
    )
    local_rows = frames * tile_h * tile_w
    wide_rows = frames * (tile_h + 2 * margin) * (tile_w + 2 * margin)
    query_rows = queries.reshape(local_rows, heads, depth)
    key_local = cache_keys.reshape(local_rows, heads, depth)
    value_local = cache_values.reshape(local_rows, heads, depth)
    upstream = grad_attended.reshape(local_rows, heads, depth)
    key_mask = with_frames(
        jnp.transpose(spatial, (0, 2, 1)), live_frames(frame_count, own_block, frames)
    )
    bundle = jnp.concatenate([cache_keys, cache_values, queries, grad_attended], axis=4)

    def forward_step(carried, tile, block_id):

        def forward_run(current):
            top, total, accum = current
            key_rows = tile[..., :width].reshape(wide_rows, heads, depth)
            value_rows = tile[..., width : 2 * width].reshape(wide_rows, heads, depth)
            allowed = with_frames(spatial, live_frames(frame_count, block_id, frames))
            score = (
                jnp.einsum("qhd,khd->hqk", query_rows, key_rows, preferred_element_type=jnp.float32)
                * scale
            )
            score = jnp.where(allowed, score, -jnp.inf)
            new_top = jnp.maximum(top, jnp.max(score, axis=2))
            weight = jnp.exp(score - new_top[:, :, None])
            fading = jnp.exp(top - new_top)
            total = total * fading + jnp.sum(weight, axis=2)
            accum = accum * fading[:, :, None] + jnp.einsum(
                "hqk,khd->hqd",
                weight.astype(jnp.bfloat16),
                value_rows,
                preferred_element_type=jnp.float32,
            )
            return (new_top, total, accum)

        active = (block_id >= 0) & (block_id <= own_block)
        return lax.cond(active, forward_run, lambda current: current, carried)

    def query_grad_step(carried, tile, block_id):

        def query_run(current):
            key_rows = tile[..., :width].reshape(wide_rows, heads, depth)
            value_rows = tile[..., width : 2 * width].reshape(wide_rows, heads, depth)
            allowed = with_frames(spatial, live_frames(frame_count, block_id, frames))
            score = (
                jnp.einsum("qhd,khd->hqk", query_rows, key_rows, preferred_element_type=jnp.float32)
                * scale
            )
            prob = jnp.exp(jnp.where(allowed, score - log_total[:, :, None], -jnp.inf))
            push = jnp.einsum(
                "qhd,khd->hqk", upstream, value_rows, preferred_element_type=jnp.float32
            )
            slope = (prob * (push - delta[:, :, None])).astype(jnp.bfloat16)
            return current + jnp.einsum(
                "hqk,khd->hqd", slope, key_rows, preferred_element_type=jnp.float32
            )

        active = (block_id >= 0) & (block_id <= own_block)
        return lax.cond(active, query_run, lambda current: current, carried)

    def key_grad_step(carried, tile, block_id):

        def key_run(current):
            grad_k, grad_v = current
            asking = tile[..., -2 * width : -width].reshape(wide_rows, heads, depth)
            asking_grad = tile[..., -width:].reshape(wide_rows, heads, depth)
            stat_tile = lax.dynamic_index_in_dim(
                stats_all, jnp.clip(block_id, 0, block_total - 1), 0, keepdims=False
            )
            stat_rows = stat_tile.reshape(wide_rows, 2 * heads)
            row_lse = jnp.transpose(stat_rows[:, :heads])
            row_delta = jnp.transpose(stat_rows[:, heads:])
            score = (
                jnp.einsum("qhd,khd->hqk", asking, key_local, preferred_element_type=jnp.float32)
                * scale
            )
            prob = jnp.exp(jnp.where(key_mask, score - row_lse[:, :, None], -jnp.inf))
            grad_v = grad_v + jnp.einsum(
                "hqk,qhd->khd",
                prob.astype(jnp.bfloat16),
                asking_grad,
                preferred_element_type=jnp.float32,
            )
            push = jnp.einsum(
                "qhd,khd->hqk", asking_grad, value_local, preferred_element_type=jnp.float32
            )
            slope = (prob * (push - row_delta[:, :, None])).astype(jnp.bfloat16)
            grad_k = grad_k + jnp.einsum(
                "hqk,qhd->khd", slope, asking, preferred_element_type=jnp.float32
            )
            return (grad_k, grad_v)

        active = (block_id >= own_block) & (block_id < block_total)
        return lax.cond(active, key_run, lambda current: current, carried)

    start_state = (
        jnp.full((heads, local_rows), -jnp.inf, jnp.float32),
        jnp.zeros((heads, local_rows), jnp.float32),
        jnp.zeros((heads, local_rows, depth), jnp.float32),
    )
    everything = lax.all_gather(bundle, "span", axis=0, tiled=True)
    wide_all = padded(everything, (("ha", 2), ("wa", 3)), RMAX)
    top, total, accum = over_tiles(forward_step, start_state, wide_all)
    attended_rows = jnp.transpose((accum / total[:, :, None]).astype(jnp.bfloat16), (1, 0, 2))
    log_total = top + jnp.log(total)
    delta = jnp.einsum("qhd,qhd->hq", upstream, attended_rows, preferred_element_type=jnp.float32)
    stats = jnp.concatenate([jnp.transpose(log_total), jnp.transpose(delta)], axis=1)
    stats = stats.reshape(1, frames, tile_h, tile_w, 2 * heads)
    stat_wide = padded(stats, (("ha", 2), ("wa", 3)), RMAX)
    stats_all = lax.all_gather(stat_wide, "span", axis=0, tiled=True)
    query_start = jnp.zeros((heads, local_rows, depth), jnp.float32)
    key_start = (
        jnp.zeros((local_rows, heads, depth), jnp.float32),
        jnp.zeros((local_rows, heads, depth), jnp.float32),
    )
    grad_q = over_tiles(query_grad_step, query_start, wide_all)
    grad_k, grad_v = over_tiles(key_grad_step, key_start, wide_all)
    final = (1, frames, tile_h, tile_w, width)
    attended = attended_rows.reshape(final)
    grad_queries = jnp.transpose(grad_q * scale, (1, 0, 2)).astype(jnp.bfloat16).reshape(final)
    grad_keys = (grad_k * scale).astype(jnp.bfloat16).reshape(final)
    grad_values = grad_v.astype(jnp.bfloat16).reshape(final)
    return (attended, grad_queries, grad_keys, grad_values)


def solution(mesh):
    placed = (
        P("span", None, "ha", "wa", None),
        P("span", None, "ha", "wa", None),
        P("span", None, "ha", "wa", None),
        P("span", None, "ha", "wa", None),
        P(),
        P(),
    )
    return jax.shard_map(
        shards,
        mesh=mesh,
        in_specs=placed,
        out_specs=(
            P("span", None, "ha", "wa", None),
            P("span", None, "ha", "wa", None),
            P("span", None, "ha", "wa", None),
            P("span", None, "ha", "wa", None),
        ),
        check_vma=False,
    )
```

profile of v0, /device:TPU:2, one launch (start us, length us, event | category | flops | bytes accessed | tf_op | source)
XLA Modules:
  0.0 646.9 jit_solution(17913290227682815183)
XLA Ops:
  7.2 2.6 pad_maximum_fusion.4
  9.8 84.9 %all-gather.2.cloned.1.call-done = bf16[8,3,4,12,3072]{4,2,3,1,0:T(4,128)(2,1)} async-done(((bf16[1,3,4,12,3072]{4,2,3,1,0:T(4,128)(2,1)}), bf16[8,3,4,12,3072]{4,2,3,1,0:T(4,128)(2,1)}) %all-gather.2.cloned.1.call-update) | async-done | bytes 7077904 | tf_op jit(solution)/shard_map/all_gather | solution.py:184
  94.7 9.5 %fusion.57 = (bf16[8,3,2,12,3072]{4,2,3,1,0:T(2,128)(2,1)S(1)}, bf16[8,3,2,12,3072]{4,2,3,1,0:T(2,128)(2,1)S(1)}) fusion(bf16[8,3,4,12,3072]{4,2,3,1,0:T(4,128)(2,1)} %all-gather.2.cloned.1.call-done), kind=kLoop, calls=%fused_computation.100 | loop fusion | bytes 14155776 | tf_op jit(solution)/shard_map/slice | solution.py:16
  104.3 1.9 copy.85
  106.2 1.9 collective-permute-start
  108.2 3.8 copy.86
  112.0 4.4 collective-permute-start.1
  116.3 32.7 %collective-permute-done = bf16[8,3,2,12,3072]{4,0,3,2,1:T(8,128)(2,1)S(1)} collective-permute-done((bf16[8,3,2,12,3072]{4,0,3,2,1:T(8,128)(2,1)S(1)}, bf16[8,3,2,12,3072]{4,0,3,2,1:T(8,128)(2,1)S(1)}, u32[]{:S(2)}, u32[]{:S(2)}) %collective-permute-start) | collective-permute-done | bytes 3538976 | tf_op jit(solution)/shard_map/ppermute | solution.py:15
  149.0 3.6 copy.87
  152.7 2.5 collective-permute-done.1
  155.2 5.6 copy.88
  160.9 5.3 pad_maximum_fusion.3
  166.2 4.8 collective-permute-start.2
  175.4 2.0 reshape.221
  179.1 2.0 reshape.223
  184.8 1.9 reshape.225
  188.4 1.9 reshape.228
  198.0 22.7 %collective-permute-done.2 = bf16[8,3,8,2,3072]{4,2,3,1,0:T(8,128)(2,1)} collective-permute-done((bf16[8,3,8,2,3072]{4,2,3,1,0:T(8,128)(2,1)}, bf16[8,3,8,2,3072]{4,2,3,1,0:T(8,128)(2,1)}, u32[]{:S(2)}, u32[]{:S(2)}) %collective-permute-start.2) | collective-permute-done | bytes 2359328 | tf_op jit(solution)/shard_map/ppermute | solution.py:15
  220.7 6.0 collective-permute-done.3
  226.8 13.9 %pad_maximum_fusion = bf16[8,3,8,16,3072]{4,2,3,1,0:T(8,128)(2,1)S(1)} fusion(bf16[8,3,8,2,3072]{4,2,3,1,0:T(8,128)(2,1)} %collective-permute-done.3, bf16[8,3,2,12,3072]{4,2,3,1,0:T(2,128)(2,1)} %copy-done, bf16[8,3,4,12,3072]{4,2,3,1,0:T(4,128)(2,1)} %all-gather.2.cloned.1.call-done, bf16[8,3,2,12,3072]{4,2,3,1,0:T(2,128)(2,1)S(1)} %copy.87, ...), kind=kLoop, calls=%fused_computation.67 | loop fusion | flops 94371840 | bytes 37748736 | tf_op jit(solution)/shard_map/concatenate | solution.py:19
  240.7 12.6 %copy.90 = bf16[8,3,8,16,3072]{4,3,2,1,0:T(8,128)(2,1)} copy(bf16[8,3,8,16,3072]{4,2,3,1,0:T(8,128)(2,1)S(1)} %pad_maximum_fusion) | data formatting | bytes 37748736
  253.4 26.6 %while.42 = (s32[]{:T(128)}, f32[6,144]{1,0:T(8,128)S(1)}, f32[6,144]{1,0:T(8,128)S(1)}, f32[6,144,128]{2,1,0:T(8,128)S(1)}, s32[8]{0:T(128)S(1)}, /*index=5*/s3...) while((s32[]{:T(128)}, f32[6,144]{1,0:T(8,128)S(1)}, ...), condition=%wide.region_6.7_spmd.clone, body=%wide.region_0.6_spmd.clone.sunk | while | flops 172599008 | bytes 17480200 | solution.py:60
  255.3 11.1 %conditional.9 = ((f32[6,144]{1,0:T(8,128)S(1)}, f32[6,144]{1,0:T(8,128)S(1)}, f32[6,144,128]{2,1,0:T(8,128)S(1)})) conditional(s32[]{:T(128)} %convert_element_type.76, (f32[6,144]{1,0:T(8,128)S(1)}, f32[6,144]{1,0:T(8,128)S(1)}, f32[6,144,128]{2,1,0:T(8,128)S(1)}) %tuple.115, (s32[4,12,8,16]{3,2,1,0:T(8,128)S(1)}, s32[]{:T(128)}, s32[8]{0:T(128)}, ...), branch_computations={%region_1.1_spmd, %region_2.0_spmd} | conditional | flops 172599008 | bytes 17479918 | solution.py:120
  282.9 2.2 collective-permute-start.4
  285.1 3.5 collective-permute-start.5
  290.0 29.6 %while.43 = (s32[]{:T(128)}, f32[6,144,128]{2,1,0:T(8,128)}, s32[8]{0:T(128)}, s32[]{:T(128)}, s32[8]{0:T(128)}, /*index=5*/bf16[8,3,8,16,3072]{4,3,2,1,0:T(8,12...) while((s32[]{:T(128)}, f32[6,144,128]{2,1,0:T(8,128)}, ...), condition=%wide.region_11.12_spmd.clone, body=%wide.region_7.11_spmd.clone.sunk | while | flops 257089568 | bytes 18095392 | solution.py:60
  292.3 11.0 %conditional.10 = (f32[6,144,128]{2,1,0:T(8,128)}) conditional(s32[]{:T(128)} %convert_element_type.77, f32[6,144,128]{2,1,0:T(8,128)} %get-tuple-element.945, (s32[4,12,8,16]{3,2,1,0:T(8,128)S(1)}, s32[]{:T(128)}, s32[8]{0:T(128)}, bf16[8,3,8,16,3072]{4,3,2,1,0:T(8,128)(2,1)}, s32[]{:T(128)}, /*index=5*/bf16[144,6,128]{2,0,1:T(8,128)(2,1)}, ...), branch_computations={%region_8.8_spmd, %region_9.10_spmd} | conditional | flops 257089568 | bytes 18095118 | solution.py:142
  300.6 2.7 fusion.23
  320.7 2.0 collective-permute-start.6
  327.4 2.8 collective-permute-done.7
  331.2 180.3 %all_gather.7 = f32[8,3,8,16,12]{3,2,4,1,0:T(8,128)S(1)} all-gather(f32[1,3,8,16,12]{3,2,4,1,0:T(8,128)S(1)} %copy.99), channel_id=1, replica_groups=mesh['span'=8,'ha'=8,'wa'=4] {'span'}, dimensions={0}, use_global_device_ids=true | all-gather | bytes 165888 | tf_op jit(solution)/shard_map/all_gather | solution.py:193
  513.5 122.9 %while.44 = (s32[]{:T(128)}, f32[144,6,128]{2,0,1:T(8,128)S(1)}, f32[144,6,128]{2,0,1:T(8,128)}, s32[8]{0:T(128)S(1)}, s32[]{:T(128)}, /*index=5*/bf16[8,3,8,16,...) while((s32[]{:T(128)}, f32[144,6,128]{2,0,1:T(8,128)S(1)}, ...), condition=%wide.region_16.17_spmd.clone, body=%wide.region_13.16_spmd.clone.sunk | while | flops 342282240 | bytes 23095652 | solution.py:60
  515.4 13.5 %conditional.11 = ((f32[144,6,128]{2,0,1:T(8,128)S(1)}, f32[144,6,128]{2,0,1:T(8,128)})) conditional(s32[]{:T(128)} %convert_element_type.78, (f32[144,6,128]{2,0,1:T(8,128)S(1)}, f32[144,6,128]{2,0,1:T(8,128)}) %tuple.120, (bf16[8,3,8,16,3072]{4,3,2,1,0:T(8,128)(2,1)}, s32[]{:T(128)}, bf16[144,6,128]{2,0,1:T(8,128)(2,1)}, s32[]{:T(128)}, ...), branch_computations={%region_14.14_spmd, %region_15.15_spmd} | conditional | flops 342282240 | bytes 23095408 | solution.py:177
  515.4 2.0 dynamic-slice_bitcast_fusion.2
  524.1 2.6 fusion.40
  526.6 2.2 fusion.41
  530.8 13.5 %conditional.11 = ((f32[144,6,128]{2,0,1:T(8,128)S(1)}, f32[144,6,128]{2,0,1:T(8,128)})) conditional(s32[]{:T(128)} %convert_element_type.78, (f32[144,6,128]{2,0,1:T(8,128)S(1)}, f32[144,6,128]{2,0,1:T(8,128)}) %tuple.120, (bf16[8,3,8,16,3072]{4,3,2,1,0:T(8,128)(2,1)}, s32[]{:T(128)}, bf16[144,6,128]{2,0,1:T(8,128)(2,1)}, s32[]{:T(128)}, ...), branch_computations={%region_14.14_spmd, %region_15.15_spmd} | conditional | flops 342282240 | bytes 23095408 | solution.py:177
  530.8 2.0 dynamic-slice_bitcast_fusion.2
  539.4 2.6 fusion.40
  542.0 2.2 fusion.41
  546.1 13.5 %conditional.11 = ((f32[144,6,128]{2,0,1:T(8,128)S(1)}, f32[144,6,128]{2,0,1:T(8,128)})) conditional(s32[]{:T(128)} %convert_element_type.78, (f32[144,6,128]{2,0,1:T(8,128)S(1)}, f32[144,6,128]{2,0,1:T(8,128)}) %tuple.120, (bf16[8,3,8,16,3072]{4,3,2,1,0:T(8,128)(2,1)}, s32[]{:T(128)}, bf16[144,6,128]{2,0,1:T(8,128)(2,1)}, s32[]{:T(128)}, ...), branch_computations={%region_14.14_spmd, %region_15.15_spmd} | conditional | flops 342282240 | bytes 23095408 | solution.py:177
  546.1 2.0 dynamic-slice_bitcast_fusion.2
  554.8 2.6 fusion.40
  557.4 2.2 fusion.41
  561.5 13.5 %conditional.11 = ((f32[144,6,128]{2,0,1:T(8,128)S(1)}, f32[144,6,128]{2,0,1:T(8,128)})) conditional(s32[]{:T(128)} %convert_element_type.78, (f32[144,6,128]{2,0,1:T(8,128)S(1)}, f32[144,6,128]{2,0,1:T(8,128)}) %tuple.120, (bf16[8,3,8,16,3072]{4,3,2,1,0:T(8,128)(2,1)}, s32[]{:T(128)}, bf16[144,6,128]{2,0,1:T(8,128)(2,1)}, s32[]{:T(128)}, ...), branch_computations={%region_14.14_spmd, %region_15.15_spmd} | conditional | flops 342282240 | bytes 23095408 | solution.py:177
  561.5 2.0 dynamic-slice_bitcast_fusion.2
  570.2 2.6 fusion.40
  572.7 2.2 fusion.41
  576.9 13.5 %conditional.11 = ((f32[144,6,128]{2,0,1:T(8,128)S(1)}, f32[144,6,128]{2,0,1:T(8,128)})) conditional(s32[]{:T(128)} %convert_element_type.78, (f32[144,6,128]{2,0,1:T(8,128)S(1)}, f32[144,6,128]{2,0,1:T(8,128)}) %tuple.120, (bf16[8,3,8,16,3072]{4,3,2,1,0:T(8,128)(2,1)}, s32[]{:T(128)}, bf16[144,6,128]{2,0,1:T(8,128)(2,1)}, s32[]{:T(128)}, ...), branch_computations={%region_14.14_spmd, %region_15.15_spmd} | conditional | flops 342282240 | bytes 23095408 | solution.py:177
  576.9 2.0 dynamic-slice_bitcast_fusion.2
  585.5 2.6 fusion.40
  588.1 2.2 fusion.41
  592.2 13.5 %conditional.11 = ((f32[144,6,128]{2,0,1:T(8,128)S(1)}, f32[144,6,128]{2,0,1:T(8,128)})) conditional(s32[]{:T(128)} %convert_element_type.78, (f32[144,6,128]{2,0,1:T(8,128)S(1)}, f32[144,6,128]{2,0,1:T(8,128)}) %tuple.120, (bf16[8,3,8,16,3072]{4,3,2,1,0:T(8,128)(2,1)}, s32[]{:T(128)}, bf16[144,6,128]{2,0,1:T(8,128)(2,1)}, s32[]{:T(128)}, ...), branch_computations={%region_14.14_spmd, %region_15.15_spmd} | conditional | flops 342282240 | bytes 23095408 | solution.py:177
  592.2 2.0 dynamic-slice_bitcast_fusion.2
  600.9 2.6 fusion.40
  603.5 2.2 fusion.41
  607.6 13.5 %conditional.11 = ((f32[144,6,128]{2,0,1:T(8,128)S(1)}, f32[144,6,128]{2,0,1:T(8,128)})) conditional(s32[]{:T(128)} %convert_element_type.78, (f32[144,6,128]{2,0,1:T(8,128)S(1)}, f32[144,6,128]{2,0,1:T(8,128)}) %tuple.120, (bf16[8,3,8,16,3072]{4,3,2,1,0:T(8,128)(2,1)}, s32[]{:T(128)}, bf16[144,6,128]{2,0,1:T(8,128)(2,1)}, s32[]{:T(128)}, ...), branch_computations={%region_14.14_spmd, %region_15.15_spmd} | conditional | flops 342282240 | bytes 23095408 | solution.py:177
  607.6 2.0 dynamic-slice_bitcast_fusion.2
  616.3 2.6 fusion.40
  618.8 2.2 fusion.41
  622.9 13.5 %conditional.11 = ((f32[144,6,128]{2,0,1:T(8,128)S(1)}, f32[144,6,128]{2,0,1:T(8,128)})) conditional(s32[]{:T(128)} %convert_element_type.78, (f32[144,6,128]{2,0,1:T(8,128)S(1)}, f32[144,6,128]{2,0,1:T(8,128)}) %tuple.120, (bf16[8,3,8,16,3072]{4,3,2,1,0:T(8,128)(2,1)}, s32[]{:T(128)}, bf16[144,6,128]{2,0,1:T(8,128)(2,1)}, s32[]{:T(128)}, ...), branch_computations={%region_14.14_spmd, %region_15.15_spmd} | conditional | flops 342282240 | bytes 23095408 | solution.py:177
  623.0 2.0 dynamic-slice_bitcast_fusion.2
  631.6 2.6 fusion.40
  634.2 2.2 fusion.41
  (267 shorter events, 121.1 us)
Async XLA Ops:
  7.2 87.6 %all-gather.2.cloned.1.call-start = ((), (), s32[]{:S(2)}) async-start(), calls=%async_computation | async-start | bytes 7962624 | tf_op jit(solution)/shard_map/all_gather | solution.py:184
  106.2 42.8 %collective-permute-start = (bf16[8,3,2,12,3072]{4,0,3,2,1:T(8,128)(2,1)S(1)}, bf16[8,3,2,12,3072]{4,0,3,2,1:T(8,128)(2,1)S(1)}, u32[]{:S(2)}, u32[]{:S(2)}) collective-permute-start(bf16[8,3,2,12,3072]{4,0,3,2,1:T(8,128)(2,1)S(1)} %copy.85), channel_id=1, source_target_pairs={{0,4},{4,8},{8,12},{12,16},{16,20},{20,24},{24,28},{1,5},{5,9},{9,... | collective-permute-start | bytes 10616840 | tf_op jit(solution)/shard_map/ppermute | solution.py:15
  108.1 52.7 %slice-start = ((s8[7077888]{0:T(1024)(128)(4,1)}), s8[4194304]{0:T(1024)(128)(4,1)S(1)}, s32[]{:S(2)}) async-start(s8[7077888]{0:T(1024)(128)(4,1)} %bitcast.91), calls=%async_computation.1 | async-start | bytes 8388608
  112.0 48.9 %slice-start.1 = ((s8[7077888]{0:T(1024)(128)(4,1)}), s8[2883584]{0:T(1024)(128)(4,1)S(1)}, s32[]{:S(2)}) async-start(s8[7077888]{0:T(1024)(128)(4,1)} %bitcast.91), calls=%async_computation.2 | async-start | bytes 5767168
  112.0 43.2 %collective-permute-start.1 = (bf16[8,3,2,12,3072]{4,0,3,2,1:T(8,128)(2,1)}, bf16[8,3,2,12,3072]{4,0,3,2,1:T(8,128)(2,1)}, u32[]{:S(2)}, u32[]{:S(2)}) collective-permute-start(bf16[8,3,2,12,3072]{4,0,3,2,1:T(8,128)(2,1)} %copy.86), channel_id=1, source_target_pairs={{4,0},{8,4},{12,8},{16,12},{20,16},{24,20},{28,24},{5,1},{9,5},{13... | collective-permute-start | bytes 10616840 | tf_op jit(solution)/shard_map/ppermute | solution.py:18
  160.8 5.3 copy-start
  160.8 11.6 %copy-start.5 = (bf16[1,3,4,12,768]{4,2,3,1,0:T(4,128)(2,1)S(1)}, bf16[1,3,4,12,768]{4,2,3,1,0:T(4,128)(2,1)}, u32[]{:S(2)}) copy-start(bf16[1,3,4,12,768]{4,2,3,1,0:T(4,128)(2,1)} %param.18) | copy-start | bytes 663556
  160.9 12.3 %copy-start.6 = (bf16[1,3,4,12,768]{4,2,3,1,0:T(4,128)(2,1)S(1)}, bf16[1,3,4,12,768]{4,2,3,1,0:T(4,128)(2,1)}, u32[]{:S(2)}) copy-start(bf16[1,3,4,12,768]{4,2,3,1,0:T(4,128)(2,1)} %param.21) | copy-start | bytes 663556
  160.9 13.0 %copy-start.7 = (bf16[1,3,4,12,768]{4,2,3,1,0:T(4,128)(2,1)S(1)}, bf16[1,3,4,12,768]{4,2,3,1,0:T(4,128)(2,1)}, u32[]{:S(2)}) copy-start(bf16[1,3,4,12,768]{4,2,3,1,0:T(4,128)(2,1)} %param.19) | copy-start | bytes 663556
  160.9 13.8 %copy-start.8 = (bf16[1,3,4,12,768]{4,2,3,1,0:T(4,128)(2,1)S(1)}, bf16[1,3,4,12,768]{4,2,3,1,0:T(4,128)(2,1)}, u32[]{:S(2)}) copy-start(bf16[1,3,4,12,768]{4,2,3,1,0:T(4,128)(2,1)} %param.20) | copy-start | bytes 663556
  166.2 54.5 %collective-permute-start.2 = (bf16[8,3,8,2,3072]{4,2,3,1,0:T(8,128)(2,1)}, bf16[8,3,8,2,3072]{4,2,3,1,0:T(8,128)(2,1)}, u32[]{:S(2)}, u32[]{:S(2)}) collective-permute-start(bf16[8,3,8,2,3072]{4,2,3,1,0:T(8,128)(2,1)} %get-tuple-element.644), channel_id=1, source_target_pairs={{0,1},{1,2},{2,3},{4,5},{5,6},{6,7},{8,9},{9,10},{10,11},{12,13},{... | collective-permute-start | bytes 7077896 | tf_op jit(solution)/shard_map/ppermute | solution.py:15
  170.9 55.8 %collective-permute-start.3 = (bf16[8,3,8,2,3072]{4,2,3,1,0:T(8,128)(2,1)}, bf16[8,3,8,2,3072]{4,2,3,1,0:T(8,128)(2,1)}, u32[]{:S(2)}, u32[]{:S(2)}) collective-permute-start(bf16[8,3,8,2,3072]{4,2,3,1,0:T(8,128)(2,1)} %get-tuple-element.645), channel_id=1, source_target_pairs={{1,0},{2,1},{3,2},{5,4},{6,5},{7,6},{9,8},{10,9},{11,10},{13,12},{... | collective-permute-start | bytes 7077896 | tf_op jit(solution)/shard_map/ppermute | solution.py:18
  175.4 21.0 %copy-start.11 = (s32[6]{0:T(128)S(1)}, s32[6]{0:T(128)}, u32[]{:S(2)}) copy-start(s32[6]{0:T(128)} %param.22) | copy-start | bytes 76
  183.2 10.6 %copy-start.12 = (pred[128]{0:T(512)(128)(4,1)S(1)}, pred[128]{0:T(512)(128)(4,1)}, u32[]{:S(2)}) copy-start(pred[128]{0:T(512)(128)(4,1)} %and.135) | copy-start | bytes 388
  240.7 12.7 %copy-start.1 = (s32[4,12,8,16]{3,2,1,0:T(8,128)S(1)}, s32[4,12,8,16]{3,2,1,0:T(8,128)}, u32[]{:S(2)}) copy-start(s32[4,12,8,16]{3,2,1,0:T(8,128)} %broadcast_maximum_fusion) | copy-start | bytes 73732
  282.9 36.7 %collective-permute-start.4 = (f32[1,3,2,12,12]{3,2,1,4,0:T(2,128)}, f32[1,3,2,12,12]{3,2,1,4,0:T(2,128)}, u32[]{:S(2)}, u32[]{:S(2)}) collective-permute-start(f32[1,3,2,12,12]{3,2,1,4,0:T(2,128)} %get-tuple-element.652), channel_id=1, source_target_pairs={{0,4},{4,8},{8,12},{12,16},{16,20},{20,24},{24,28},{1,5},{5,9},{9,... | collective-permute-start | bytes 10376 | tf_op jit(solution)/shard_map/ppermute | solution.py:15
  285.1 34.5 %collective-permute-start.5 = (f32[1,3,2,12,12]{3,2,1,4,0:T(2,128)}, f32[1,3,2,12,12]{3,2,1,4,0:T(2,128)}, u32[]{:S(2)}, u32[]{:S(2)}) collective-permute-start(f32[1,3,2,12,12]{3,2,1,4,0:T(2,128)} %get-tuple-element.653), channel_id=1, source_target_pairs={{4,0},{8,4},{12,8},{16,12},{20,16},{24,20},{28,24},{5,1},{9,5},{13... | collective-permute-start | bytes 10376 | tf_op jit(solution)/shard_map/ppermute | solution.py:18
  294.1 0.9 copy-start.4
  295.5 5.1 copy-start.10
  319.6 6.6 %copy-start.9 = (bf16[144,6,128]{2,0,1:T(8,128)(2,1)S(1)}, bf16[144,6,128]{2,0,1:T(8,128)(2,1)}, u32[]{:S(2)}) copy-start(bf16[144,6,128]{2,0,1:T(8,128)(2,1)} %get-tuple-element.649) | copy-start | bytes 663556
  320.7 6.7 %collective-permute-start.6 = (f32[1,3,8,2,12]{3,2,1,4,0:T(8,128)S(1)}, f32[1,3,8,2,12]{3,2,1,4,0:T(8,128)S(1)}, u32[]{:S(2)}, u32[]{:S(2)}) collective-permute-start(f32[1,3,8,2,12]{3,2,1,4,0:T(8,128)S(1)} %get-tuple-element.650), channel_id=1, source_target_pairs={{0,1},{1,2},{2,3},{4,5},{5,6},{6,7},{8,9},{9,10},{10,11},{12,13},{... | collective-permute-start | bytes 6920 | tf_op jit(solution)/shard_map/ppermute | solution.py:15
  322.7 7.5 %collective-permute-start.7 = (f32[1,3,8,2,12]{3,2,1,4,0:T(8,128)S(1)}, f32[1,3,8,2,12]{3,2,1,4,0:T(8,128)S(1)}, u32[]{:S(2)}, u32[]{:S(2)}) collective-permute-start(f32[1,3,8,2,12]{3,2,1,4,0:T(8,128)S(1)} %get-tuple-element.651), channel_id=1, source_target_pairs={{1,0},{2,1},{3,2},{5,4},{6,5},{7,6},{9,8},{10,9},{11,10},{13,12},{... | collective-permute-start | bytes 6920 | tf_op jit(solution)/shard_map/ppermute | solution.py:18
  515.4 2.0 copy-start.2
  526.6 2.2 copy-start.3
  530.8 2.0 copy-start.2
  542.0 2.2 copy-start.3
  546.1 2.0 copy-start.2
  557.4 2.2 copy-start.3
  561.5 2.0 copy-start.2
  572.7 2.2 copy-start.3
  576.9 2.0 copy-start.2
  588.1 2.2 copy-start.3
  592.2 2.0 copy-start.2
  603.5 2.2 copy-start.3
  607.6 2.0 copy-start.2
  618.8 2.2 copy-start.3
  623.0 2.0 copy-start.2
  634.2 2.2 copy-start.3
Sparse Core Ops, SparseCore 0:
  10.0 84.7 all-gather.1
where the time goes:
time: 655 us; the launch traced here: 647 us
  blocking collectives  180 us (27%)
  waiting for transfers between devices  152 us (23%)
  local copies, waits for them, and re-layouts  147 us (22%)
  matrix products  55.1 us (8%)
  other arithmetic  39.6 us (6%)
  loops' own time  36.7 us (6%)
  starting transfers between devices  21.6 us (3%)
  between operations  14.7 us (2%)
    all_gather x1, blocking collectives, shards(): stats_all = lax.all_gather(stat_wide, 'span', axis=0, tiled=True)  180 us
    all_gather x1, waiting for transfers between devices, shards(): everything = lax.all_gather(bundle, 'span', axis=0, tiled=True)  84.9 us
    ppermute x4, waiting for transfers between devices, padded(): lax.ppermute(lax.slice_in_dim(block, block.shape[dim] - width, None, axis...  55.4 us
    another operation x3, loops' own time, over_tiles(): result, _ = lax.scan(inner, carried, (piece, block_ids))  30.3 us
    unnamed x36, local copies, waits for them, and re-layouts  26.6 us
    dot_general x8, matrix products, key_run(): jnp.einsum('hqk,qhd->khd', slope, asking, preferred_element_type=jnp.floa...  20.5 us
    squeeze x10, local copies, waits for them, and re-layouts, over_tiles(): result, _ = lax.scan(inner, carried, (piece, block_ids))  19.7 us
    dynamic_slice x24, local copies, waits for them, and re-layouts, over_tiles(): result, _ = lax.scan(inner, carried, (piece, block_ids))  18.6 us
  transfers between devices with their start and end apart: 9, of which 6 were waited for; matrix products, arithmetic and copies ran while one was open for 9% of the time, Pallas kernels for 0%

commit v1 on v0

--- a/solution.py
+++ b/solution.py
@@ -190,7 +190,10 @@
     stats = jnp.concatenate([jnp.transpose(log_total), jnp.transpose(delta)], axis=1)
     stats = stats.reshape(1, frames, tile_h, tile_w, 2 * heads)
     stat_wide = padded(stats, (("ha", 2), ("wa", 3)), RMAX)
-    stats_all = lax.all_gather(stat_wide, "span", axis=0, tiled=True)
+    n_dev = lax.axis_size("span")
+    tiles = jnp.stack([stat_wide for _ in range(n_dev)])
+    tiles = lax.all_to_all(tiles, "span", split_axis=0, concat_axis=0)
+    stats_all = jnp.concatenate(tiles, axis=0)
     query_start = jnp.zeros((heads, local_rows, depth), jnp.float32)
     key_start = (
         jnp.zeros((local_rows, heads, depth), jnp.float32),

time: 655 us -> 558 us (0.85)
  blocking collectives: 180 us -> 0 us
  starting transfers between devices: 21.6 us -> 99.4 us
  waiting for transfers between devices: 152 us -> 168 us
  local copies, waits for them, and re-layouts: 147 us -> 135 us
    all_gather x1 -> x0, blocking collectives: 180 us -> none  [shards(): stats_all = lax.all_gather(stat_wide, 'span', axis=0, tiled=True)]
    all_to_all x0 -> x1, starting transfers between devices: none -> 77.7 us  [shards(): tiles = lax.all_to_all(tiles, 'span', split_axis=0, concat_axis=0)]
    ppermute x4, waiting for transfers between devices: 55.4 us -> 69.2 us  [padded(): lax.ppermute(lax.slice_in_dim(block, block.shape[dim] - width, None, axis...]
    unnamed x36 -> x42, local copies, waits for them, and re-layouts: 26.6 us -> 22.2 us
  transfers between devices with their start and end apart: 9 -> 10, of which waited for: 6 -> 8; matrix products, arithmetic and copies ran while one was open for 9% -> 8% of each run, Pallas kernels for 0% -> 0%
where the time goes in v1:
time: 558 us; the launch traced here: 550 us
  waiting for transfers between devices  168 us (30%)
  local copies, waits for them, and re-layouts  135 us (24%)
  starting transfers between devices  99.4 us (18%)
  matrix products  55.2 us (10%)
  other arithmetic  38.9 us (7%)
  loops' own time  38 us (7%)
  between operations  14.7 us (3%)
    all_gather x1, waiting for transfers between devices, shards(): everything = lax.all_gather(bundle, 'span', axis=0, tiled=True)  84.9 us
    all_to_all x1, starting transfers between devices, shards(): tiles = lax.all_to_all(tiles, 'span', split_axis=0, concat_axis=0)  77.7 us
    ppermute x4, waiting for transfers between devices, padded(): lax.ppermute(lax.slice_in_dim(block, block.shape[dim] - width, None, axis...  69.2 us
    another operation x3, loops' own time, over_tiles(): result, _ = lax.scan(inner, carried, (piece, block_ids))  31.6 us
    unnamed x42, local copies, waits for them, and re-layouts  22.2 us
    dot_general x8, matrix products, key_run(): jnp.einsum('hqk,qhd->khd', slope, asking, preferred_element_type=jnp.floa...  20.6 us
    squeeze x10, local copies, waits for them, and re-layouts, over_tiles(): result, _ = lax.scan(inner, carried, (piece, block_ids))  19.7 us
    dot_general x8, matrix products, key_run(): jnp.einsum('hqk,qhd->khd', prob.astype(jnp.bfloat16), asking_grad, prefer...  17.8 us
  transfers between devices with their start and end apart: 10, of which 8 were waited for; matrix products, arithmetic and copies ran while one was open for 8% of the time, Pallas kernels for 0%

profile of v1, /device:TPU:2, one launch (start us, length us, event | category | flops | bytes accessed | tf_op | source)
XLA Modules:
  0.0 549.8 jit_solution(8473128701877446615)
XLA Ops:
  7.2 2.6 pad_maximum_fusion.4
  9.9 84.9 %all-gather.2.cloned.1.call-done = bf16[8,3,4,12,3072]{4,2,3,1,0:T(4,128)(2,1)} async-done(((bf16[1,3,4,12,3072]{4,2,3,1,0:T(4,128)(2,1)}), bf16[8,3,4,12,3072]{4,2,3,1,0:T(4,128)(2,1)}) %all-gather.2.cloned.1.call-update) | async-done | bytes 7077904 | tf_op jit(solution)/shard_map/all_gather | solution.py:184
  94.7 9.5 %fusion.57 = (bf16[8,3,2,12,3072]{4,2,3,1,0:T(2,128)(2,1)S(1)}, bf16[8,3,2,12,3072]{4,2,3,1,0:T(2,128)(2,1)S(1)}) fusion(bf16[8,3,4,12,3072]{4,2,3,1,0:T(4,128)(2,1)} %all-gather.2.cloned.1.call-done), kind=kLoop, calls=%fused_computation.100 | loop fusion | bytes 14155776 | tf_op jit(solution)/shard_map/slice | solution.py:16
  104.2 1.9 copy.51
  106.2 1.9 collective-permute-start
  108.1 3.8 copy.52
  112.0 4.4 collective-permute-start.1
  116.3 32.7 %collective-permute-done = bf16[8,3,2,12,3072]{4,0,3,2,1:T(8,128)(2,1)S(1)} collective-permute-done((bf16[8,3,2,12,3072]{4,0,3,2,1:T(8,128)(2,1)S(1)}, bf16[8,3,2,12,3072]{4,0,3,2,1:T(8,128)(2,1)S(1)}, u32[]{:S(2)}, u32[]{:S(2)}) %collective-permute-start) | collective-permute-done | bytes 3538976 | tf_op jit(solution)/shard_map/ppermute | solution.py:15
  149.0 3.6 copy.53
  152.6 2.5 collective-permute-done.1
  155.2 5.6 %copy.54 = bf16[8,3,2,12,3072]{4,2,3,1,0:T(2,128)(2,1)S(1)} copy(bf16[8,3,2,12,3072]{4,0,3,2,1:T(8,128)(2,1)} %collective-permute-done.1) | data formatting | bytes 7077888 | tf_op jit(solution)/shard_map/ppermute | solution.py:18
  160.9 5.3 pad_maximum_fusion.3
  166.1 4.9 collective-permute-start.2
  174.0 1.9 reshape.227
  177.6 1.9 reshape.229
  185.6 35.2 %collective-permute-done.2 = bf16[8,3,8,2,3072]{4,2,3,1,0:T(8,128)(2,1)} collective-permute-done((bf16[8,3,8,2,3072]{4,2,3,1,0:T(8,128)(2,1)}, bf16[8,3,8,2,3072]{4,2,3,1,0:T(8,128)(2,1)}, u32[]{:S(2)}, u32[]{:S(2)}) %collective-permute-start.2) | collective-permute-done | bytes 2359328 | tf_op jit(solution)/shard_map/ppermute | solution.py:15
  220.8 6.0 %collective-permute-done.3 = bf16[8,3,8,2,3072]{4,2,3,1,0:T(8,128)(2,1)} collective-permute-done((bf16[8,3,8,2,3072]{4,2,3,1,0:T(8,128)(2,1)}, bf16[8,3,8,2,3072]{4,2,3,1,0:T(8,128)(2,1)}, u32[]{:S(2)}, u32[]{:S(2)}) %collective-permute-start.3) | collective-permute-done | bytes 2359328 | tf_op jit(solution)/shard_map/ppermute | solution.py:18
  226.9 13.9 %pad_maximum_fusion = bf16[8,3,8,16,3072]{4,2,3,1,0:T(8,128)(2,1)S(1)} fusion(bf16[8,3,8,2,3072]{4,2,3,1,0:T(8,128)(2,1)} %collective-permute-done.3, bf16[8,3,2,12,3072]{4,2,3,1,0:T(2,128)(2,1)} %copy-done, bf16[8,3,4,12,3072]{4,2,3,1,0:T(4,128)(2,1)} %all-gather.2.cloned.1.call-done, bf16[8,3,2,12,3072]{4,2,3,1,0:T(2,128)(2,1)S(1)} %copy.53, ...), kind=kLoop, calls=%fused_computation.67 | loop fusion | flops 94371840 | bytes 37748736 | tf_op jit(solution)/shard_map/concatenate | solution.py:19
  240.8 12.6 %copy.56 = bf16[8,3,8,16,3072]{4,3,2,1,0:T(8,128)(2,1)} copy(bf16[8,3,8,16,3072]{4,2,3,1,0:T(8,128)(2,1)S(1)} %pad_maximum_fusion) | data formatting | bytes 37748736
  253.5 26.1 %while.42 = (s32[]{:T(128)}, f32[6,144]{1,0:T(8,128)S(1)}, f32[6,144]{1,0:T(8,128)S(1)}, f32[6,144,128]{2,1,0:T(8,128)S(1)}, s32[8]{0:T(128)S(1)}, /*index=5*/s3...) while((s32[]{:T(128)}, f32[6,144]{1,0:T(8,128)S(1)}, ...), condition=%wide.region_6.7_spmd.clone, body=%wide.region_0.6_spmd.clone.sunk | while | flops 172599008 | bytes 17480200 | solution.py:60
  255.4 10.7 %conditional.9 = ((f32[6,144]{1,0:T(8,128)S(1)}, f32[6,144]{1,0:T(8,128)S(1)}, f32[6,144,128]{2,1,0:T(8,128)S(1)})) conditional(s32[]{:T(128)} %convert_element_type.76, (f32[6,144]{1,0:T(8,128)S(1)}, f32[6,144]{1,0:T(8,128)S(1)}, f32[6,144,128]{2,1,0:T(8,128)S(1)}) %tuple.111, (s32[4,12,8,16]{3,2,1,0:T(8,128)S(1)}, s32[]{:T(128)}, s32[8]{0:T(128)S(1)}, ...), branch_computations={%region_1.1_spmd, %region_2.0_spmd} | conditional | flops 172599008 | bytes 17479918 | solution.py:120
  255.4 1.8 dynamic-slice_bitcast_fusion
  282.0 2.4 collective-permute-start.4
  284.4 3.3 collective-permute-start.5
  289.5 2.0 collective-permute-start.6
  294.9 4.7 collective-permute-done.7
  301.0 77.7 %all-to-all-start = ((f32[8,1,4608]{2,1,0:T(1,128)}), f32[8,1,4608]{2,1,0:T(1,128)}, u32[]{:S(2)}, u32[]{:S(2)}) async-start(f32[8,1,4608]{2,1,0:T(1,128)} %reshape.246), calls=%async_computation | async-start | bytes 294912 | tf_op jit(solution)/shard_map/all_to_all | solution.py:195
  382.4 25.7 %while.43 = (s32[]{:T(128)}, f32[6,144,128]{2,1,0:T(8,128)}, s32[8]{0:T(128)S(1)}, s32[]{:T(128)}, s32[8]{0:T(128)S(1)}, /*index=5*/bf16[8,3,8,16,3072]{4,3,2,1,...) while((s32[]{:T(128)}, f32[6,144,128]{2,1,0:T(8,128)}, ...), condition=%wide.region_11.12_spmd.clone, body=%wide.region_7.11_spmd.clone.sunk | while | flops 257089568 | bytes 16325865 | solution.py:60
  384.2 10.4 %conditional.10 = (f32[6,144,128]{2,1,0:T(8,128)}) conditional(s32[]{:T(128)} %convert_element_type.77, f32[6,144,128]{2,1,0:T(8,128)} %get-tuple-element.906, (s32[4,12,8,16]{3,2,1,0:T(8,128)S(1)}, s32[]{:T(128)}, s32[8]{0:T(128)S(1)}, bf16[8,3,8,16,3072]{4,3,2,1,0:T(8,128)(2,1)}, s32[]{:T(128)}, /*index=5*/bf16[144,6,128]{2,0,1:T(8,128)(2,1)}, ...), branch_computations={%region_8.8_spmd, %region_9.10_spmd} | conditional | flops 257089568 | bytes 16325590 | solution.py:142
  391.9 2.8 fusion.23
  412.1 1.9 reduce.2
  416.3 122.9 %while.44 = (s32[]{:T(128)}, f32[144,6,128]{2,0,1:T(8,128)S(1)}, f32[144,6,128]{2,0,1:T(8,128)}, s32[8]{0:T(128)S(1)}, s32[]{:T(128)}, /*index=5*/bf16[8,3,8,16,...) while((s32[]{:T(128)}, f32[144,6,128]{2,0,1:T(8,128)S(1)}, ...), condition=%wide.region_16.17_spmd.clone, body=%wide.region_13.16_spmd.clone.sunk | while | flops 342282240 | bytes 23095652 | solution.py:60
  418.2 13.5 %conditional.11 = ((f32[144,6,128]{2,0,1:T(8,128)S(1)}, f32[144,6,128]{2,0,1:T(8,128)})) conditional(s32[]{:T(128)} %convert_element_type.78, (f32[144,6,128]{2,0,1:T(8,128)S(1)}, f32[144,6,128]{2,0,1:T(8,128)}) %tuple.116, (bf16[8,3,8,16,3072]{4,3,2,1,0:T(8,128)(2,1)}, s32[]{:T(128)}, bf16[144,6,128]{2,0,1:T(8,128)(2,1)}, s32[]{:T(128)}, ...), branch_computations={%region_14.14_spmd, %region_15.15_spmd} | conditional | flops 342282240 | bytes 23095408 | solution.py:177
  418.3 2.0 dynamic-slice_bitcast_fusion.2
  426.9 2.6 fusion.40
  429.5 2.2 fusion.41
  433.6 13.5 %conditional.11 = ((f32[144,6,128]{2,0,1:T(8,128)S(1)}, f32[144,6,128]{2,0,1:T(8,128)})) conditional(s32[]{:T(128)} %convert_element_type.78, (f32[144,6,128]{2,0,1:T(8,128)S(1)}, f32[144,6,128]{2,0,1:T(8,128)}) %tuple.116, (bf16[8,3,8,16,3072]{4,3,2,1,0:T(8,128)(2,1)}, s32[]{:T(128)}, bf16[144,6,128]{2,0,1:T(8,128)(2,1)}, s32[]{:T(128)}, ...), branch_computations={%region_14.14_spmd, %region_15.15_spmd} | conditional | flops 342282240 | bytes 23095408 | solution.py:177
  433.6 2.0 dynamic-slice_bitcast_fusion.2
  442.3 2.6 fusion.40
  444.8 2.2 fusion.41
  448.9 13.5 %conditional.11 = ((f32[144,6,128]{2,0,1:T(8,128)S(1)}, f32[144,6,128]{2,0,1:T(8,128)})) conditional(s32[]{:T(128)} %convert_element_type.78, (f32[144,6,128]{2,0,1:T(8,128)S(1)}, f32[144,6,128]{2,0,1:T(8,128)}) %tuple.116, (bf16[8,3,8,16,3072]{4,3,2,1,0:T(8,128)(2,1)}, s32[]{:T(128)}, bf16[144,6,128]{2,0,1:T(8,128)(2,1)}, s32[]{:T(128)}, ...), branch_computations={%region_14.14_spmd, %region_15.15_spmd} | conditional | flops 342282240 | bytes 23095408 | solution.py:177
  449.0 2.0 dynamic-slice_bitcast_fusion.2
  457.6 2.6 fusion.40
  460.2 2.2 fusion.41
  464.3 13.5 %conditional.11 = ((f32[144,6,128]{2,0,1:T(8,128)S(1)}, f32[144,6,128]{2,0,1:T(8,128)})) conditional(s32[]{:T(128)} %convert_element_type.78, (f32[144,6,128]{2,0,1:T(8,128)S(1)}, f32[144,6,128]{2,0,1:T(8,128)}) %tuple.116, (bf16[8,3,8,16,3072]{4,3,2,1,0:T(8,128)(2,1)}, s32[]{:T(128)}, bf16[144,6,128]{2,0,1:T(8,128)(2,1)}, s32[]{:T(128)}, ...), branch_computations={%region_14.14_spmd, %region_15.15_spmd} | conditional | flops 342282240 | bytes 23095408 | solution.py:177
  464.3 2.0 dynamic-slice_bitcast_fusion.2
  473.0 2.6 fusion.40
  475.6 2.2 fusion.41
  479.7 13.5 %conditional.11 = ((f32[144,6,128]{2,0,1:T(8,128)S(1)}, f32[144,6,128]{2,0,1:T(8,128)})) conditional(s32[]{:T(128)} %convert_element_type.78, (f32[144,6,128]{2,0,1:T(8,128)S(1)}, f32[144,6,128]{2,0,1:T(8,128)}) %tuple.116, (bf16[8,3,8,16,3072]{4,3,2,1,0:T(8,128)(2,1)}, s32[]{:T(128)}, bf16[144,6,128]{2,0,1:T(8,128)(2,1)}, s32[]{:T(128)}, ...), branch_computations={%region_14.14_spmd, %region_15.15_spmd} | conditional | flops 342282240 | bytes 23095408 | solution.py:177
  479.7 2.0 dynamic-slice_bitcast_fusion.2
  488.4 2.6 fusion.40
  490.9 2.2 fusion.41
  495.1 13.5 %conditional.11 = ((f32[144,6,128]{2,0,1:T(8,128)S(1)}, f32[144,6,128]{2,0,1:T(8,128)})) conditional(s32[]{:T(128)} %convert_element_type.78, (f32[144,6,128]{2,0,1:T(8,128)S(1)}, f32[144,6,128]{2,0,1:T(8,128)}) %tuple.116, (bf16[8,3,8,16,3072]{4,3,2,1,0:T(8,128)(2,1)}, s32[]{:T(128)}, bf16[144,6,128]{2,0,1:T(8,128)(2,1)}, s32[]{:T(128)}, ...), branch_computations={%region_14.14_spmd, %region_15.15_spmd} | conditional | flops 342282240 | bytes 23095408 | solution.py:177
  495.1 2.0 dynamic-slice_bitcast_fusion.2
  503.7 2.6 fusion.40
  506.3 2.2 fusion.41
  510.4 13.5 %conditional.11 = ((f32[144,6,128]{2,0,1:T(8,128)S(1)}, f32[144,6,128]{2,0,1:T(8,128)})) conditional(s32[]{:T(128)} %convert_element_type.78, (f32[144,6,128]{2,0,1:T(8,128)S(1)}, f32[144,6,128]{2,0,1:T(8,128)}) %tuple.116, (bf16[8,3,8,16,3072]{4,3,2,1,0:T(8,128)(2,1)}, s32[]{:T(128)}, bf16[144,6,128]{2,0,1:T(8,128)(2,1)}, s32[]{:T(128)}, ...), branch_computations={%region_14.14_spmd, %region_15.15_spmd} | conditional | flops 342282240 | bytes 23095408 | solution.py:177
  510.4 2.0 dynamic-slice_bitcast_fusion.2
  519.1 2.6 fusion.40
  521.7 2.2 fusion.41
  525.8 13.5 %conditional.11 = ((f32[144,6,128]{2,0,1:T(8,128)S(1)}, f32[144,6,128]{2,0,1:T(8,128)})) conditional(s32[]{:T(128)} %convert_element_type.78, (f32[144,6,128]{2,0,1:T(8,128)S(1)}, f32[144,6,128]{2,0,1:T(8,128)}) %tuple.116, (bf16[8,3,8,16,3072]{4,3,2,1,0:T(8,128)(2,1)}, s32[]{:T(128)}, bf16[144,6,128]{2,0,1:T(8,128)(2,1)}, s32[]{:T(128)}, ...), branch_computations={%region_14.14_spmd, %region_15.15_spmd} | conditional | flops 342282240 | bytes 23095408 | solution.py:177
  525.8 2.0 dynamic-slice_bitcast_fusion.2
  534.5 2.6 fusion.40
  537.0 2.2 fusion.41
  (272 shorter events, 110.8 us)
Async XLA Ops:
  7.2 87.6 %all-gather.2.cloned.1.call-start = ((), (), s32[]{:S(2)}) async-start(), calls=%async_computation.1 | async-start | bytes 7962624 | tf_op jit(solution)/shard_map/all_gather | solution.py:184
  106.2 42.8 %collective-permute-start = (bf16[8,3,2,12,3072]{4,0,3,2,1:T(8,128)(2,1)S(1)}, bf16[8,3,2,12,3072]{4,0,3,2,1:T(8,128)(2,1)S(1)}, u32[]{:S(2)}, u32[]{:S(2)}) collective-permute-start(bf16[8,3,2,12,3072]{4,0,3,2,1:T(8,128)(2,1)S(1)} %copy.51), channel_id=1, source_target_pairs={{0,4},{4,8},{8,12},{12,16},{16,20},{20,24},{24,28},{1,5},{5,9},{9,... | collective-permute-start | bytes 10616840 | tf_op jit(solution)/shard_map/ppermute | solution.py:15
  108.1 52.7 %slice-start = ((s8[7077888]{0:T(1024)(128)(4,1)}), s8[4194304]{0:T(1024)(128)(4,1)S(1)}, s32[]{:S(2)}) async-start(s8[7077888]{0:T(1024)(128)(4,1)} %bitcast.99), calls=%async_computation.2 | async-start | bytes 8388608
  112.0 48.9 %slice-start.1 = ((s8[7077888]{0:T(1024)(128)(4,1)}), s8[2883584]{0:T(1024)(128)(4,1)S(1)}, s32[]{:S(2)}) async-start(s8[7077888]{0:T(1024)(128)(4,1)} %bitcast.99), calls=%async_computation.3 | async-start | bytes 5767168
  112.0 43.2 %collective-permute-start.1 = (bf16[8,3,2,12,3072]{4,0,3,2,1:T(8,128)(2,1)}, bf16[8,3,2,12,3072]{4,0,3,2,1:T(8,128)(2,1)}, u32[]{:S(2)}, u32[]{:S(2)}) collective-permute-start(bf16[8,3,2,12,3072]{4,0,3,2,1:T(8,128)(2,1)} %copy.52), channel_id=1, source_target_pairs={{4,0},{8,4},{12,8},{16,12},{20,16},{24,20},{28,24},{5,1},{9,5},{13... | collective-permute-start | bytes 10616840 | tf_op jit(solution)/shard_map/ppermute | solution.py:18
  160.8 5.3 copy-start
  160.8 11.7 %copy-start.5 = (bf16[1,3,4,12,768]{4,2,3,1,0:T(4,128)(2,1)S(1)}, bf16[1,3,4,12,768]{4,2,3,1,0:T(4,128)(2,1)}, u32[]{:S(2)}) copy-start(bf16[1,3,4,12,768]{4,2,3,1,0:T(4,128)(2,1)} %param.18) | copy-start | bytes 663556
  160.8 12.4 %copy-start.6 = (bf16[1,3,4,12,768]{4,2,3,1,0:T(4,128)(2,1)S(1)}, bf16[1,3,4,12,768]{4,2,3,1,0:T(4,128)(2,1)}, u32[]{:S(2)}) copy-start(bf16[1,3,4,12,768]{4,2,3,1,0:T(4,128)(2,1)} %param.21) | copy-start | bytes 663556
  166.1 18.0 %copy-start.11 = (s32[6]{0:T(128)S(1)}, s32[6]{0:T(128)}, u32[]{:S(2)}) copy-start(s32[6]{0:T(128)} %param.22) | copy-start | bytes 76
  166.1 54.7 %collective-permute-start.2 = (bf16[8,3,8,2,3072]{4,2,3,1,0:T(8,128)(2,1)}, bf16[8,3,8,2,3072]{4,2,3,1,0:T(8,128)(2,1)}, u32[]{:S(2)}, u32[]{:S(2)}) collective-permute-start(bf16[8,3,8,2,3072]{4,2,3,1,0:T(8,128)(2,1)} %get-tuple-element.605), channel_id=1, source_target_pairs={{0,1},{1,2},{2,3},{4,5},{5,6},{6,7},{8,9},{9,10},{10,11},{12,13},{... | collective-permute-start | bytes 7077896 | tf_op jit(solution)/shard_map/ppermute | solution.py:15
  171.0 55.8 %collective-permute-start.3 = (bf16[8,3,8,2,3072]{4,2,3,1,0:T(8,128)(2,1)}, bf16[8,3,8,2,3072]{4,2,3,1,0:T(8,128)(2,1)}, u32[]{:S(2)}, u32[]{:S(2)}) collective-permute-start(bf16[8,3,8,2,3072]{4,2,3,1,0:T(8,128)(2,1)} %get-tuple-element.606), channel_id=1, source_target_pairs={{1,0},{2,1},{3,2},{5,4},{6,5},{7,6},{9,8},{10,9},{11,10},{13,12},{... | collective-permute-start | bytes 7077896 | tf_op jit(solution)/shard_map/ppermute | solution.py:18
  240.8 12.7 %copy-start.1 = (s32[4,12,8,16]{3,2,1,0:T(8,128)S(1)}, s32[4,12,8,16]{3,2,1,0:T(8,128)}, u32[]{:S(2)}) copy-start(s32[4,12,8,16]{3,2,1,0:T(8,128)} %broadcast_maximum_fusion) | copy-start | bytes 73732
  240.8 12.7 %copy-start.12 = (s32[8]{0:T(128)S(1)}, s32[8]{0:T(128)}, u32[]{:S(2)}) copy-start(s32[8]{0:T(128)} %param.23) | copy-start | bytes 100
  281.8 96.8 %copy-start.10 = (pred[6,128,48]{1,2,0:T(8,128)(4,1)S(1)}, pred[6,128,48]{1,2,0:T(8,128)(4,1)}, u32[]{:S(2)}) copy-start(pred[6,128,48]{1,2,0:T(8,128)(4,1)} %compare_and_fusion.2) | copy-start | bytes 110596
  282.0 97.5 %copy-start.7 = (bf16[1,3,4,12,768]{4,2,3,1,0:T(4,128)(2,1)S(1)}, bf16[1,3,4,12,768]{4,2,3,1,0:T(4,128)(2,1)}, u32[]{:S(2)}) copy-start(bf16[1,3,4,12,768]{4,2,3,1,0:T(4,128)(2,1)} %param.19) | copy-start | bytes 663556
  282.0 6.3 %collective-permute-start.4 = (f32[1,3,2,12,12]{3,2,1,4,0:T(2,128)S(1)}, f32[1,3,2,12,12]{3,2,1,4,0:T(2,128)S(1)}, u32[]{:S(2)}, u32[]{:S(2)}) collective-permute-start(f32[1,3,2,12,12]{3,2,1,4,0:T(2,128)S(1)} %get-tuple-element.613), channel_id=1, source_target_pairs={{0,4},{4,8},{8,12},{12,16},{16,20},{20,24},{24,28},{1,5},{5,9},{9,... | collective-permute-start | bytes 10376 | tf_op jit(solution)/shard_map/ppermute | solution.py:15
  284.4 5.0 collective-permute-start.5
  289.4 90.1 %copy-start.8 = (bf16[1,3,4,12,768]{4,2,3,1,0:T(4,128)(2,1)S(1)}, bf16[1,3,4,12,768]{4,2,3,1,0:T(4,128)(2,1)}, u32[]{:S(2)}) copy-start(bf16[1,3,4,12,768]{4,2,3,1,0:T(4,128)(2,1)} %param.20) | copy-start | bytes 663556
  289.5 5.3 collective-permute-start.6
  291.6 8.0 %collective-permute-start.7 = (f32[1,3,8,2,12]{3,2,1,4,0:T(8,128)S(1)}, f32[1,3,8,2,12]{3,2,1,4,0:T(8,128)S(1)}, u32[]{:S(2)}, u32[]{:S(2)}) collective-permute-start(f32[1,3,8,2,12]{3,2,1,4,0:T(8,128)S(1)} %get-tuple-element.612), channel_id=1, source_target_pairs={{1,0},{2,1},{3,2},{5,4},{6,5},{7,6},{9,8},{10,9},{11,10},{13,12},{... | collective-permute-start | bytes 6920 | tf_op jit(solution)/shard_map/ppermute | solution.py:18
  293.5 86.0 %copy-start.4 = (bf16[144,6,128]{2,1,0:T(8,128)(2,1)S(1)}, bf16[144,6,128]{2,1,0:T(8,128)(2,1)}, u32[]{:S(2)}) copy-start(bf16[144,6,128]{2,1,0:T(8,128)(2,1)} %reshape.229) | copy-start | bytes 663556
  301.0 110.6 %all-to-all-start = ((f32[8,1,4608]{2,1,0:T(1,128)}), f32[8,1,4608]{2,1,0:T(1,128)}, u32[]{:S(2)}, u32[]{:S(2)}) async-start(f32[8,1,4608]{2,1,0:T(1,128)} %reshape.246), calls=%async_computation | async-start | bytes 294912 | tf_op jit(solution)/shard_map/all_to_all | solution.py:195
  408.1 2.3 copy-start.9
  418.2 2.0 copy-start.2
  429.5 2.2 copy-start.3
  433.6 2.0 copy-start.2
  444.8 2.2 copy-start.3
  449.0 2.0 copy-start.2
  460.2 2.2 copy-start.3
  464.3 2.0 copy-start.2
  475.6 2.2 copy-start.3
  479.7 2.0 copy-start.2
  490.9 2.2 copy-start.3
  495.1 2.0 copy-start.2
  506.3 2.2 copy-start.3
  510.4 2.0 copy-start.2
  521.7 2.2 copy-start.3
  525.8 2.0 copy-start.2
  537.0 2.2 copy-start.3
Sparse Core Ops, SparseCore 0:
  10.0 84.7 all-gather.1
